TPU v7x, 32 devices: a whole 2x2x4 slice. The times are simulated.
32 devices in a mesh: row: 8 (over z, y), col: 4 (over x, core).
Axes of the slice: x: 2, y: 2, z: 4, core: 2. Of those that a mesh axis runs over, the one named last changes fastest.
Arguments:
- tokens: bfloat16 [384, 8192], P('row', 'col'), may hold values from -6 to 6
- weight: bfloat16 [8192, 32768], P('col', 'row'), may hold values from -0.109375 to 0.109375
- tile_rows: int32 [8, 4, 256], P('row', 'col'), may hold values from 0 to 63, as said below
- tile_cols: int32 [8, 4, 256], P('row', 'col'), may hold values from 0 to 255, as said below
- tile_count: int32 [8, 4], P('row', 'col'), may hold values from 64 to 256, as said below
- hidden_cotangent: bfloat16 [384, 32768], P('col', 'row'), may hold values from -6 to 6
Outputs:
- hidden: bfloat16 [384, 32768], P('col', 'row')
- input_grad: bfloat16 [384, 8192], P('row', 'col')
- weight_grad: bfloat16 [8192, 32768], P('col', 'row')
Inputs may be any that keep to these rules, and one draw needn't show every extreme that they name: tile_rows[r, c, k] is a row block of the weight (tiles of 128 x 128) among the 16 blocks from c * 16 on, which index c of col holds. tile_cols[r, c, k] is a column block among the 32 blocks from r * 32 on, which index r of row holds; the 256 candidate tiles of one device are distinct. The first tile_count[r, c] candidates of device (r, c) are its nonzero tiles; some device holds 256.
All inputs are finite; a program needn't handle non-finite values.
Results may differ from a plain program's by a relative error of at most 0.0049.
Values may be sent and summed in bfloat16 or wider, within the bound.
A program may use at most 128 MiB of HBM per device.

v0:
```python
import jax
import jax.numpy as jnp
from jax import lax
from jax.sharding import PartitionSpec as P

TILE = 128


def sparse_apply(inputs, live_tiles, in_index, out_index, out_blocks, flipped):
    count_rows, in_width = inputs.shape
    in_blocks = in_width // TILE
    block_rows = 128
    picker = (in_index[:, None] == jnp.arange(in_blocks)[None, :]).astype(jnp.bfloat16)
    placer = (out_index[:, None] == jnp.arange(out_blocks)[None, :]).astype(jnp.float32)

    def per_block(rows_block):
        shaped_rows = rows_block.reshape(block_rows, in_blocks, TILE)
        pieces = jnp.einsum(
            "bjp,kj->bkp", shaped_rows, picker, preferred_element_type=jnp.float32
        ).astype(jnp.bfloat16)
        if flipped:
            product = jnp.einsum(
                "bkq,kpq->bkp", pieces, live_tiles, preferred_element_type=jnp.float32
            )
        else:
            product = jnp.einsum(
                "bkp,kpq->bkq", pieces, live_tiles, preferred_element_type=jnp.float32
            )
        placed = jnp.einsum("bkq,kc->bcq", product, placer, precision=lax.Precision.HIGHEST)
        return placed.reshape(block_rows, out_blocks * TILE)

    stacked = inputs.reshape(count_rows // block_rows, block_rows, in_width)
    return lax.map(per_block, stacked).reshape(count_rows, out_blocks * TILE)


def tile_grads(full_tokens, full_grads, local_rows, local_cols, is_live, row_blocks, col_blocks):
    count_rows = full_tokens.shape[0]
    block_rows = 128
    steps_count = count_rows // block_rows
    left_side = full_tokens.reshape(steps_count, block_rows, row_blocks, TILE)
    right_side = full_grads.reshape(steps_count, block_rows, col_blocks, TILE)

    def accumulate(running, block_pair):
        token_block, grad_block = block_pair
        product = jnp.einsum(
            "bkp,bkq->kpq",
            token_block[:, local_rows],
            grad_block[:, local_cols],
            preferred_element_type=jnp.float32,
        )
        return (running + product, None)

    start_sums = jnp.zeros((local_rows.shape[0], TILE, TILE), jnp.float32)
    tile_sums, leftover = lax.scan(accumulate, start_sums, (left_side, right_side))
    tile_sums = tile_sums * is_live[:, None, None].astype(jnp.float32)
    slot_ids = local_rows * col_blocks + local_cols
    placed = (
        jnp.zeros((row_blocks * col_blocks, TILE, TILE), jnp.float32).at[slot_ids].add(tile_sums)
    )
    placed = placed.reshape(row_blocks, col_blocks, TILE, TILE).transpose(0, 2, 1, 3)
    return placed.reshape(row_blocks * TILE, col_blocks * TILE).astype(jnp.bfloat16)


def on_device(tokens, weight, tile_rows, tile_cols, tile_count, hidden_cotangent):
    row_index = lax.axis_index("row")
    col_index = lax.axis_index("col")
    row_blocks = weight.shape[0] // TILE
    col_blocks = weight.shape[1] // TILE
    capacity = tile_rows.shape[2]
    local_rows = tile_rows.reshape(capacity) - col_index * row_blocks
    local_cols = tile_cols.reshape(capacity) - row_index * col_blocks
    is_live = jnp.arange(capacity) < tile_count.reshape(())
    shaped = weight.reshape(row_blocks, TILE, col_blocks, TILE)
    live_tiles = shaped[local_rows, :, local_cols, :] * is_live[:, None, None].astype(jnp.bfloat16)
    full_tokens = lax.all_gather(tokens, "row", axis=0, tiled=True)
    pre_act = lax.psum_scatter(
        sparse_apply(full_tokens, live_tiles, local_rows, local_cols, col_blocks, False),
        "col",
        scatter_dimension=0,
        tiled=True,
    )
    gate_value = jax.nn.sigmoid(pre_act)
    hidden = (pre_act * gate_value).astype(jnp.bfloat16)
    silu_slope = gate_value * (1.0 + pre_act * (1.0 - gate_value))
    grad_pre = (hidden_cotangent.astype(jnp.float32) * silu_slope).astype(jnp.bfloat16)
    full_grads = lax.all_gather(grad_pre, "col", axis=0, tiled=True)
    input_grad = lax.psum_scatter(
        sparse_apply(full_grads, live_tiles, local_cols, local_rows, row_blocks, True),
        "row",
        scatter_dimension=0,
        tiled=True,
    ).astype(jnp.bfloat16)
    weight_grad = tile_grads(
        full_tokens, full_grads, local_rows, local_cols, is_live, row_blocks, col_blocks
    )
    return (hidden, input_grad, weight_grad)


def solution(mesh):
    in_specs = (
        P("row", "col"),
        P("col", "row"),
        P("row", "col", None),
        P("row", "col", None),
        P("row", "col"),
        P("col", "row"),
    )
    out_specs = (P("col", "row"), P("row", "col"), P("col", "row"))
    return jax.shard_map(
        on_device, mesh=mesh, in_specs=in_specs, out_specs=out_specs, check_vma=False
    )
```

profile of v0, /device:TPU:0, one launch (start us, length us, event | category | flops | bytes accessed | tf_op | source)
XLA Modules:
  0.0 783.4 jit_solution(11281175233865779121)
XLA Ops:
  8.6 9.7 %copy.25 = bf16[256,8,32,128]{3,2,1,0:T(8,128)(2,1)S(1)} copy(bf16[256,8,32,128]{3,1,2,0:T(8,128)(2,1)} %bitcast.159) | data formatting | bytes 33554432
  18.3 8.9 %copy.16 = bf16[16,128,32,128]{3,1,2,0:T(8,128)(2,1)} copy(bf16[16,128,32,128]{3,2,1,0:T(8,128)(2,1)S(1)} %bitcast.153) | data formatting | bytes 33554432 | tf_op jit(solution)/shard_map/reshape | solution.py:73
  27.8 16.0 %gather_fusion.2 = bf16[256,128,128]{2,1,0:T(8,128)(2,1)} fusion(bf16[16,128,32,128]{3,1,2,0:T(8,128)(2,1)} %copy.16, s32[256]{0:T(256)S(1)} %bitcast.158), kind=kCustom, calls=%fused_computation.2 | custom fusion | bytes 16779264 | tf_op jit(solution)/shard_map/gather | solution.py:74
  43.8 7.4 broadcast_multiply_fusion.1
  51.2 5.9 all-gather.3.cloned.1.call-done
  57.1 187.1 %while.33 = (s32[]{:T(128)}, f32[3,128,4096]{2,1,0:T(8,128)}, bf16[3,128,2048]{2,1,0:T(8,128)(2,1)}, bf16[256,128,128]{2,1,0:T(8,128)(2,1)}, s32[256]{0:T(256)S(1)}, /*index=5*/s32[256]{0:T(256)S(1)}, s32[]{:T(128)}) while((s32[]{:T(128)}, f32[3,128,4096]{2,1,0:T(8,128)}, bf16[3,128,2048]{2,1,0:T(8,128)(2,1)}, ...), condition=%wide.region_1.2_spmd.clone, body=%wide.region_0.1_spmd.clone.sunk | while | flops 2822791168 | bytes 88606816 | solution.py:33
  58.5 5.8 convert_bitcast_fusion.4
  64.3 12.3 %copy.53 = bf16[128,256,128]{2,0,1:T(8,128)(2,1)} copy(bf16[128,256,128]{1,2,0:T(8,128)(2,1)} %convert_bitcast_fusion.4) | data formatting | bytes 16777216 | tf_op jit(solution)/shard_map/while/body/eval_jaxpr/convert_element_type | solution.py:20
  76.6 14.4 %convolution_bitcast_fusion.4 = f32[128,256,128]{2,0,1:T(8,128)} fusion(bf16[128,256,128]{2,0,1:T(8,128)(2,1)} %copy.53, bf16[256,128,128]{2,1,0:T(8,128)(2,1)} %get-tuple-element.338), kind=kOutput, calls=%fused_computation.10.clone.1 | convolution fusion | flops 1073741824 | bytes 33554432 | tf_op jit(solution)/shard_map/while/body/eval_jaxpr/bkp,kpq->bkq/dot_general | solution.py:26
  91.0 23.9 %fusion.69 = f32[128,32,128]{2,1,0:T(8,128)S(1)} fusion(f32[128,256,128]{2,0,1:T(8,128)} %convolution_bitcast_fusion.4, s32[256]{0:T(256)S(1)} %get-tuple-element.340), kind=kOutput, calls=%fused_computation.12.clone.1 | convolution fusion | flops 1610629120 | bytes 18875392 | tf_op jit(solution)/shard_map/while/body/eval_jaxpr/bkq,kc->bcq/dot_general | solution.py:29
  115.0 1.5 broadcast_in_dim.43
  116.5 3.1 constant_dynamic-update-slice_fusion.4
  120.8 5.8 convert_bitcast_fusion.4
  126.6 12.3 %copy.53 = bf16[128,256,128]{2,0,1:T(8,128)(2,1)} copy(bf16[128,256,128]{1,2,0:T(8,128)(2,1)} %convert_bitcast_fusion.4) | data formatting | bytes 16777216 | tf_op jit(solution)/shard_map/while/body/eval_jaxpr/convert_element_type | solution.py:20
  138.9 14.4 %convolution_bitcast_fusion.4 = f32[128,256,128]{2,0,1:T(8,128)} fusion(bf16[128,256,128]{2,0,1:T(8,128)(2,1)} %copy.53, bf16[256,128,128]{2,1,0:T(8,128)(2,1)} %get-tuple-element.338), kind=kOutput, calls=%fused_computation.10.clone.1 | convolution fusion | flops 1073741824 | bytes 33554432 | tf_op jit(solution)/shard_map/while/body/eval_jaxpr/bkp,kpq->bkq/dot_general | solution.py:26
  153.3 23.9 %fusion.69 = f32[128,32,128]{2,1,0:T(8,128)S(1)} fusion(f32[128,256,128]{2,0,1:T(8,128)} %convolution_bitcast_fusion.4, s32[256]{0:T(256)S(1)} %get-tuple-element.340), kind=kOutput, calls=%fused_computation.12.clone.1 | convolution fusion | flops 1610629120 | bytes 18875392 | tf_op jit(solution)/shard_map/while/body/eval_jaxpr/bkq,kc->bcq/dot_general | solution.py:29
  177.3 1.5 broadcast_in_dim.43
  178.8 3.1 constant_dynamic-update-slice_fusion.4
  183.1 5.8 convert_bitcast_fusion.4
  188.9 12.3 %copy.53 = bf16[128,256,128]{2,0,1:T(8,128)(2,1)} copy(bf16[128,256,128]{1,2,0:T(8,128)(2,1)} %convert_bitcast_fusion.4) | data formatting | bytes 16777216 | tf_op jit(solution)/shard_map/while/body/eval_jaxpr/convert_element_type | solution.py:20
  201.2 14.4 %convolution_bitcast_fusion.4 = f32[128,256,128]{2,0,1:T(8,128)} fusion(bf16[128,256,128]{2,0,1:T(8,128)(2,1)} %copy.53, bf16[256,128,128]{2,1,0:T(8,128)(2,1)} %get-tuple-element.338), kind=kOutput, calls=%fused_computation.10.clone.1 | convolution fusion | flops 1073741824 | bytes 33554432 | tf_op jit(solution)/shard_map/while/body/eval_jaxpr/bkp,kpq->bkq/dot_general | solution.py:26
  215.6 23.9 %fusion.69 = f32[128,32,128]{2,1,0:T(8,128)S(1)} fusion(f32[128,256,128]{2,0,1:T(8,128)} %convolution_bitcast_fusion.4, s32[256]{0:T(256)S(1)} %get-tuple-element.340), kind=kOutput, calls=%fused_computation.12.clone.1 | convolution fusion | flops 1610629120 | bytes 18875392 | tf_op jit(solution)/shard_map/while/body/eval_jaxpr/bkq,kc->bcq/dot_general | solution.py:29
  239.6 1.5 broadcast_in_dim.43
  241.1 3.1 constant_dynamic-update-slice_fusion.4
  244.3 57.3 %reduce-scatter.3.cloned.1.call-done = f32[96,4096]{1,0:T(8,128)} async-done(((f32[384,4096]{1,0:T(8,128)}), f32[96,4096]{1,0:T(8,128)}) %reduce-scatter.3.cloned.1.call-update) | async-done | bytes 1572880 | tf_op jit(solution)/shard_map/reduce_scatter | solution.py:76
  301.6 3.2 multiply_convert_fusion
  305.4 1.7 copy.26
  307.1 26.4 %all-gather.5.cloned.1.call-done = bf16[384,4096]{1,0:T(8,128)(2,1)} async-done(((bf16[96,4096]{1,0:T(8,128)(2,1)}), bf16[384,4096]{1,0:T(8,128)(2,1)}) %all-gather.5.cloned.1.call-update) | async-done | bytes 3145744 | tf_op jit(solution)/shard_map/all_gather | solution.py:86
  333.5 184.4 %while.34 = (s32[]{:T(128)}, f32[3,128,2048]{2,1,0:T(8,128)}, bf16[3,128,4096]{2,1,0:T(8,128)(2,1)}, bf16[256,128,128]{2,1,0:T(8,128)(2,1)}, s32[256]{0:T(256)S(1)}, /*index=5*/s32[256]{0:T(256)S(1)}, s32[]{:T(128)}) while((s32[]{:T(128)}, f32[3,128,2048]{2,1,0:T(8,128)}, bf16[3,128,4096]{2,1,0:T(8,128)(2,1)}, ...), condition=%wide.region_4.5_spmd.clone, body=%wide.region_3.4_spmd.clone.sunk | while | flops 2151702528 | bytes 85985376 | solution.py:33
  333.9 1.3 dynamic-slice_bitcast_fusion.5
  335.5 5.6 convert_bitcast_fusion.5
  341.1 12.4 %copy.56 = bf16[128,256,128]{2,0,1:T(8,128)(2,1)} copy(bf16[128,256,128]{1,2,0:T(8,128)(2,1)} %convert_bitcast_fusion.5) | data formatting | bytes 16777216 | tf_op jit(solution)/shard_map/while/body/eval_jaxpr/convert_element_type | solution.py:20
  353.5 17.4 %convolution_bitcast_fusion.5 = f32[128,256,128]{2,0,1:T(8,128)} fusion(bf16[128,256,128]{2,0,1:T(8,128)(2,1)} %copy.56, bf16[256,128,128]{2,1,0:T(8,128)(2,1)} %get-tuple-element.359), kind=kOutput, calls=%fused_computation.25.clone.1 | convolution fusion | flops 1073741824 | bytes 33554432 | tf_op jit(solution)/shard_map/while/body/eval_jaxpr/bkq,kpq->bkp/dot_general | solution.py:22
  370.9 23.1 %fusion.76 = f32[128,16,128]{2,1,0:T(8,128)S(1)} fusion(f32[128,256,128]{2,0,1:T(8,128)} %convolution_bitcast_fusion.5, s32[256]{0:T(256)S(1)} %get-tuple-element.361), kind=kOutput, calls=%fused_computation.27.clone.1 | convolution fusion | flops 805314560 | bytes 17826816 | tf_op jit(solution)/shard_map/while/body/eval_jaxpr/bkq,kc->bcq/dot_general | solution.py:29
  396.8 5.6 convert_bitcast_fusion.5
  402.4 12.4 %copy.56 = bf16[128,256,128]{2,0,1:T(8,128)(2,1)} copy(bf16[128,256,128]{1,2,0:T(8,128)(2,1)} %convert_bitcast_fusion.5) | data formatting | bytes 16777216 | tf_op jit(solution)/shard_map/while/body/eval_jaxpr/convert_element_type | solution.py:20
  414.8 17.4 %convolution_bitcast_fusion.5 = f32[128,256,128]{2,0,1:T(8,128)} fusion(bf16[128,256,128]{2,0,1:T(8,128)(2,1)} %copy.56, bf16[256,128,128]{2,1,0:T(8,128)(2,1)} %get-tuple-element.359), kind=kOutput, calls=%fused_computation.25.clone.1 | convolution fusion | flops 1073741824 | bytes 33554432 | tf_op jit(solution)/shard_map/while/body/eval_jaxpr/bkq,kpq->bkp/dot_general | solution.py:22
  432.2 23.1 %fusion.76 = f32[128,16,128]{2,1,0:T(8,128)S(1)} fusion(f32[128,256,128]{2,0,1:T(8,128)} %convolution_bitcast_fusion.5, s32[256]{0:T(256)S(1)} %get-tuple-element.361), kind=kOutput, calls=%fused_computation.27.clone.1 | convolution fusion | flops 805314560 | bytes 17826816 | tf_op jit(solution)/shard_map/while/body/eval_jaxpr/bkq,kc->bcq/dot_general | solution.py:29
  456.5 1.3 dynamic-slice_bitcast_fusion.5
  458.1 5.6 convert_bitcast_fusion.5
  463.7 12.4 %copy.56 = bf16[128,256,128]{2,0,1:T(8,128)(2,1)} copy(bf16[128,256,128]{1,2,0:T(8,128)(2,1)} %convert_bitcast_fusion.5) | data formatting | bytes 16777216 | tf_op jit(solution)/shard_map/while/body/eval_jaxpr/convert_element_type | solution.py:20
  476.1 17.4 %convolution_bitcast_fusion.5 = f32[128,256,128]{2,0,1:T(8,128)} fusion(bf16[128,256,128]{2,0,1:T(8,128)(2,1)} %copy.56, bf16[256,128,128]{2,1,0:T(8,128)(2,1)} %get-tuple-element.359), kind=kOutput, calls=%fused_computation.25.clone.1 | convolution fusion | flops 1073741824 | bytes 33554432 | tf_op jit(solution)/shard_map/while/body/eval_jaxpr/bkq,kpq->bkp/dot_general | solution.py:22
  493.5 23.1 %fusion.76 = f32[128,16,128]{2,1,0:T(8,128)S(1)} fusion(f32[128,256,128]{2,0,1:T(8,128)} %convolution_bitcast_fusion.5, s32[256]{0:T(256)S(1)} %get-tuple-element.361), kind=kOutput, calls=%fused_computation.27.clone.1 | convolution fusion | flops 805314560 | bytes 17826816 | tf_op jit(solution)/shard_map/while/body/eval_jaxpr/bkq,kc->bcq/dot_general | solution.py:29
  518.0 4.4 copy.27
  522.4 110.1 %while.35 = (s32[]{:T(128)}, f32[256,128,128]{2,1,0:T(8,128)}, bf16[3,128,16,128]{3,2,1,0:T(8,128)(2,1)}, s32[256]{0:T(256)S(1)}, bf16[3,128,32,128]{3,2,1,0:T(8...) while((s32[]{:T(128)}, f32[256,128,128]{2,1,0:T(8,128)}, ...), condition=%wide.region_7.8_spmd.clone, body=%wide.region_6.7_spmd.clone.sunk | while | flops 1082134016 | bytes 90194024 | solution.py:54
  523.7 1.3 constant_dynamic-slice_fusion.4
  525.4 8.7 %gather_fusion = bf16[256,128,128]{2,1,0:T(8,128)(2,1)} fusion(bf16[128,32,128]{2,0,1:T(8,128)(2,1)S(1)} %bitcast.149, s32[1024]{0:T(1024)S(1)} %pad_clamp_fusion.4), kind=kCustom, calls=%fused_computation.1.clone.clone.1 | custom fusion | bytes 16778240 | tf_op jit(solution)/shard_map/while/body/eval_jaxpr/gather | solution.py:48
  534.1 8.8 %gather_fusion.1 = bf16[256,128,128]{2,1,0:T(8,128)(2,1)} fusion(bf16[128,16,128]{2,0,1:T(8,128)(2,1)S(1)} %bitcast.148, s32[1024]{0:T(1024)S(1)} %pad_clamp_fusion.5), kind=kCustom, calls=%fused_computation.clone.clone.1 | custom fusion | bytes 16778240 | tf_op jit(solution)/shard_map/while/body/eval_jaxpr/gather | solution.py:47
  542.9 11.3 %select_add_fusion.2 = f32[256,128,128]{2,1,0:T(8,128)} fusion(f32[256,128,128]{2,1,0:T(8,128)} %get-tuple-element.372, bf16[256,128,128]{2,1,0:T(8,128)(2,1)} %gather_fusion, bf16[256,128,128]{2,1,0:T(8,128)(2,1)} %gather_fusion.1, pred[]{:T(512)S(6)} %compare.3), kind=kOutput, calls=%fused_computation.38.clone.1 | convolution fusion | flops 1082130432 | bytes 50331648 | tf_op jit(solution)/shard_map/while/body/eval_jaxpr/bkp,bkq->kpq/dot_general | solution.py:45
  555.5 1.3 constant_dynamic-slice_fusion.4
  557.2 8.6 %gather_fusion = bf16[256,128,128]{2,1,0:T(8,128)(2,1)} fusion(bf16[128,32,128]{2,0,1:T(8,128)(2,1)S(1)} %bitcast.149, s32[1024]{0:T(1024)S(1)} %pad_clamp_fusion.4), kind=kCustom, calls=%fused_computation.1.clone.clone.1 | custom fusion | bytes 16778240 | tf_op jit(solution)/shard_map/while/body/eval_jaxpr/gather | solution.py:48
  565.8 8.7 %gather_fusion.1 = bf16[256,128,128]{2,1,0:T(8,128)(2,1)} fusion(bf16[128,16,128]{2,0,1:T(8,128)(2,1)S(1)} %bitcast.148, s32[1024]{0:T(1024)S(1)} %pad_clamp_fusion.5), kind=kCustom, calls=%fused_computation.clone.clone.1 | custom fusion | bytes 16778240 | tf_op jit(solution)/shard_map/while/body/eval_jaxpr/gather | solution.py:47
  574.5 19.1 %select_add_fusion.2 = f32[256,128,128]{2,1,0:T(8,128)} fusion(f32[256,128,128]{2,1,0:T(8,128)} %get-tuple-element.372, bf16[256,128,128]{2,1,0:T(8,128)(2,1)} %gather_fusion, bf16[256,128,128]{2,1,0:T(8,128)(2,1)} %gather_fusion.1, pred[]{:T(512)S(6)} %compare.3), kind=kOutput, calls=%fused_computation.38.clone.1 | convolution fusion | flops 1082130432 | bytes 50331648 | tf_op jit(solution)/shard_map/while/body/eval_jaxpr/bkp,bkq->kpq/dot_general | solution.py:45
  594.8 1.3 constant_dynamic-slice_fusion.4
  596.5 8.6 %gather_fusion = bf16[256,128,128]{2,1,0:T(8,128)(2,1)} fusion(bf16[128,32,128]{2,0,1:T(8,128)(2,1)S(1)} %bitcast.149, s32[1024]{0:T(1024)S(1)} %pad_clamp_fusion.4), kind=kCustom, calls=%fused_computation.1.clone.clone.1 | custom fusion | bytes 16778240 | tf_op jit(solution)/shard_map/while/body/eval_jaxpr/gather | solution.py:48
  605.1 8.7 %gather_fusion.1 = bf16[256,128,128]{2,1,0:T(8,128)(2,1)} fusion(bf16[128,16,128]{2,0,1:T(8,128)(2,1)S(1)} %bitcast.148, s32[1024]{0:T(1024)S(1)} %pad_clamp_fusion.5), kind=kCustom, calls=%fused_computation.clone.clone.1 | custom fusion | bytes 16778240 | tf_op jit(solution)/shard_map/while/body/eval_jaxpr/gather | solution.py:47
  613.8 18.7 %select_add_fusion.2 = f32[256,128,128]{2,1,0:T(8,128)} fusion(f32[256,128,128]{2,1,0:T(8,128)} %get-tuple-element.372, bf16[256,128,128]{2,1,0:T(8,128)(2,1)} %gather_fusion, bf16[256,128,128]{2,1,0:T(8,128)(2,1)} %gather_fusion.1, pred[]{:T(512)S(6)} %compare.3), kind=kOutput, calls=%fused_computation.38.clone.1 | convolution fusion | flops 1082130432 | bytes 50331648 | tf_op jit(solution)/shard_map/while/body/eval_jaxpr/bkp,bkq->kpq/dot_general | solution.py:45
  632.5 11.8 %broadcast_multiply_fusion = f32[256,128,128]{2,1,0:T(8,128)} fusion(f32[256,128,128]{2,1,0:T(8,128)} %get-tuple-element.101, f32[256]{0:T(256)S(1)} %copy-done.3), kind=kLoop, calls=%fused_computation.50 | loop fusion | flops 4194304 | bytes 33555456 | tf_op jit(solution)/shard_map/mul | solution.py:55
  644.3 11.3 %broadcast_in_dim.17 = f32[512,128,128]{2,1,0:T(8,128)} broadcast(f32[]{:T(128)} %constant.32.clone.1), dimensions={} | broadcast | bytes 33554436 | tf_op jit(solution)/shard_map/broadcast_in_dim | solution.py:58
  655.5 52.9 %scatter_fusion = f32[512,128,128]{2,1,0:T(8,128)} fusion(f32[512,128,128]{2,1,0:T(8,128)} %broadcast_in_dim.17, s32[256]{0:T(256)S(1)} %bitcast.172, f32[256,128,128]{2,1,0:T(8,128)} %broadcast_multiply_fusion), kind=kCustom, calls=%fused_computation.3 | custom fusion | flops 4194304 | bytes 50332672 | tf_op jit(solution)/shard_map/scatter-add | solution.py:58
  708.5 12.3 %convert_element_type.74 = bf16[512,128,128]{2,1,0:T(8,128)(2,1)S(1)} convert(f32[512,128,128]{2,1,0:T(8,128)} %scatter_fusion) | non-fusion elementwise | flops 8388608 | bytes 50331648 | tf_op jit(solution)/shard_map/convert_element_type | solution.py:61
  720.8 43.2 %copy.19 = bf16[16,128,32,128]{3,2,1,0:T(8,128)(2,1)S(1)} copy(bf16[16,128,32,128]{3,1,2,0:T(8,128)(2,1)S(1)} %bitcast.151) | data formatting | bytes 33554432 | tf_op jit(solution)/shard_map/convert_element_type | solution.py:61
  764.0 11.0 %copy.42 = bf16[256,8,32,128]{3,1,2,0:T(8,128)(2,1)} copy(bf16[256,8,32,128]{3,2,1,0:T(8,128)(2,1)S(1)} %bitcast.152) | data formatting | bytes 33554432
  775.0 1.7 convert_element_type.72
  (65 shorter events, 16.3 us)
Async XLA Ops:
  7.2 49.9 %all-gather.3.cloned.1.call-start = ((), (), s32[]{:S(2)}) async-start(), calls=%async_computation.2 | async-start | bytes 1769472 | tf_op jit(solution)/shard_map/all_gather | solution.py:75
  7.9 293.7 %reduce-scatter.3.cloned.1.call-start = ((), (), s32[]{:S(2)}) async-start(), calls=%async_computation.3 | async-start | bytes 7864320 | tf_op jit(solution)/shard_map/reduce_scatter | solution.py:76
  18.3 9.0 %copy-start.4 = (s32[1,1,256]{2,1,0:T(1,128)S(1)}, s32[1,1,256]{2,1,0:T(1,128)}, u32[]{:S(2)}) copy-start(s32[1,1,256]{2,1,0:T(1,128)} %param.14) | copy-start | bytes 3076
  18.3 8.9 %copy-start.5 = (s32[1,1,256]{2,1,0:T(1,128)S(1)}, s32[1,1,256]{2,1,0:T(1,128)}, u32[]{:S(2)}) copy-start(s32[1,1,256]{2,1,0:T(1,128)} %param.15) | copy-start | bytes 3076
  57.1 244.5 %copy-start.1 = (bf16[96,4096]{1,0:T(8,128)(2,1)S(1)}, bf16[96,4096]{1,0:T(8,128)(2,1)}, u32[]{:S(2)}) copy-start(bf16[96,4096]{1,0:T(8,128)(2,1)} %param.17) | copy-start | bytes 2359300
  244.2 61.2 %copy-start = (bf16[3,128,2048]{2,1,0:T(8,128)(2,1)S(1)}, bf16[3,128,2048]{2,1,0:T(8,128)(2,1)}, u32[]{:S(2)}) copy-start(bf16[3,128,2048]{2,1,0:T(8,128)(2,1)} %get-tuple-element.395) | copy-start | bytes 4718596
  244.3 89.3 %all-gather.5.cloned.1.call-start = ((), (), s32[]{:S(2)}) async-start(), calls=%async_computation.4 | async-start | bytes 3932160 | tf_op jit(solution)/shard_map/all_gather | solution.py:86
  304.9 470.1 %reduce-scatter.5.cloned.1.call-start = ((), (), s32[]{:S(2)}) async-start(), calls=%async_computation.5 | async-start | bytes 3538944 | tf_op jit(solution)/shard_map/reduce_scatter | solution.py:87
  522.4 110.1 %copy-start.3 = (f32[256]{0:T(256)S(1)}, f32[256]{0:T(256)}, u32[]{:S(2)}) copy-start(f32[256]{0:T(256)} %fusion.39) | copy-start | bytes 3076
  644.3 11.3 %copy-start.2 = (s32[256,1]{0,1:T(1,128)S(1)}, s32[256,1]{0,1:T(1,128)}, u32[]{:S(2)}) copy-start(s32[256,1]{0,1:T(1,128)} %get-tuple-element.205) | copy-start | bytes 3076
Sparse Core Ops, SparseCore 0:
  10.2 46.9 all-gather.2
  244.4 57.1 reduce-scatter.2
  305.0 28.5 all-gather.4
  518.1 74.2 reduce-scatter.4
where the time goes:
time: 791 us; the launch traced here: 783 us
  matrix products  320 us (40%)
  local copies, waits for them, and re-layouts  267 us (34%)
  waiting for transfers between devices  90.4 us (11%)
  other arithmetic  90.4 us (11%)
  between operations  14.7 us (2%)
    dot_general x6, matrix products, per_block(): jnp.einsum('bkq,kc->bcq', product, placer, precision=lax.Precision.HIGHEST)  141 us
    convert_element_type x6, local copies, waits for them, and re-layouts, per_block(): pieces = jnp.einsum('bjp,kj->bkp', shaped_rows, picker, preferred_element...  74.1 us
    reduce_scatter x1, waiting for transfers between devices, on_device(): lax.psum_scatter(sparse_apply(full_tokens, live_tiles, local_rows, local_...  57.3 us
    scatter-add x1, other arithmetic, tile_grads(): jnp.zeros((row_blocks * col_blocks, TILE, TILE), jnp.float32).at[slot_ids]  52.9 us
    dot_general x3, matrix products, per_block(): jnp.einsum('bkq,kpq->bkp', pieces, live_tiles, preferred_element_type=jnp...  52.2 us
    dot_general x3, matrix products, accumulate(): jnp.einsum('bkp,bkq->kpq', token_block[:, local_rows], grad_block[:, loca...  49 us
    convert_element_type x1, local copies, waits for them, and re-layouts, tile_grads(): placed.reshape(row_blocks * TILE, col_blocks * TILE).astype(jnp.bfloat16)  43.2 us
    dot_general x3, matrix products, per_block(): jnp.einsum('bkp,kpq->bkq', pieces, live_tiles, preferred_element_type=jnp...  43.2 us
  transfers between devices with their start and end apart: 4, of which 3 were waited for; matrix products, arithmetic and copies ran while one was open for 38% of the time, Pallas kernels for 0%

commit v1 on v0

v1 whole, which is shorter than its diff:
```python
import jax
import jax.numpy as jnp
from jax import lax
from jax.sharding import PartitionSpec as P

TILE = 128


def exchange_sum(partial, axis):
    n = lax.psum(1, axis)
    rows = partial.shape[0] // n
    mine = lax.all_to_all(
        partial.reshape(n, rows, partial.shape[1]), axis, split_axis=0, concat_axis=0
    )
    return mine.astype(jnp.float32).sum(axis=0)


def on_device(tokens, weight, tile_rows, tile_cols, tile_count, hidden_cotangent):
    row_index = lax.axis_index("row")
    col_index = lax.axis_index("col")
    row_blocks = weight.shape[0] // TILE
    col_blocks = weight.shape[1] // TILE
    capacity = tile_rows.shape[2]
    local_rows = tile_rows.reshape(capacity) - col_index * row_blocks
    local_cols = tile_cols.reshape(capacity) - row_index * col_blocks
    is_live = jnp.arange(capacity) < tile_count.reshape(())
    row_pick = (
        (local_rows[None, :] == jnp.arange(row_blocks)[:, None]) & is_live[None, :]
    ).astype(jnp.bfloat16)
    col_pick = (local_cols[:, None] == (jnp.arange(weight.shape[1]) // TILE)[None, :]).astype(
        jnp.bfloat16
    )
    mask = jnp.dot(row_pick, col_pick, preferred_element_type=jnp.float32)
    live = (mask > 0.5)[:, None, :]
    shaped = weight.reshape(row_blocks, TILE, weight.shape[1])
    masked = jnp.where(live, shaped, jnp.zeros_like(shaped)).reshape(weight.shape)

    full_tokens = lax.all_gather(tokens, "row", axis=0, tiled=True)
    partial = jnp.dot(full_tokens, masked, preferred_element_type=jnp.float32)
    pre_act = exchange_sum(partial.astype(jnp.bfloat16), "col")
    gate_value = jax.nn.sigmoid(pre_act)
    hidden = (pre_act * gate_value).astype(jnp.bfloat16)
    silu_slope = gate_value * (1.0 + pre_act * (1.0 - gate_value))
    grad_pre = (hidden_cotangent.astype(jnp.float32) * silu_slope).astype(jnp.bfloat16)
    full_grads = lax.all_gather(grad_pre, "col", axis=0, tiled=True)
    share = lax.dot_general(
        full_grads, masked, (((1,), (1,)), ((), ())), preferred_element_type=jnp.float32
    )
    input_grad = exchange_sum(share.astype(jnp.bfloat16), "row").astype(jnp.bfloat16)
    full = lax.dot_general(
        full_tokens, full_grads, (((0,), (0,)), ((), ())), preferred_element_type=jnp.float32
    ).reshape(row_blocks, TILE, weight.shape[1])
    weight_grad = jnp.where(live, full, 0.0).astype(jnp.bfloat16).reshape(weight.shape)
    return (hidden, input_grad, weight_grad)


def solution(mesh):
    in_specs = (
        P("row", "col"),
        P("col", "row"),
        P("row", "col", None),
        P("row", "col", None),
        P("row", "col"),
        P("col", "row"),
    )
    out_specs = (P("col", "row"), P("row", "col"), P("col", "row"))
    return jax.shard_map(
        on_device, mesh=mesh, in_specs=in_specs, out_specs=out_specs, check_vma=False
    )
```

time: 791 us -> 232 us (0.29)
  matrix products: 320 us -> 45 us
  local copies, waits for them, and re-layouts: 267 us -> 71.6 us
  other arithmetic: 90.4 us -> 4.66 us
  waiting for transfers between devices: 90.4 us -> 49.8 us
  blocking collectives: 0 us -> 39.4 us
    dot_general x21 -> x4, matrix products: 320 us -> 45 us  [the longest x1 17.3 us: on_device(): lax.dot_general(full_tokens, full_grads, (((0,), (0,)), ((), ())), prefer...]
    convert_element_type x7 -> x0, local copies, waits for them, and re-layouts: 117 us -> none  [the longest x6 74.1 us: per_block(): pieces = jnp.einsum('bjp,kj->bkp', shaped_rows, picker, preferred_element...]
    gather x7 -> x0, local copies, waits for them, and re-layouts: 68 us -> none  [the longest x3 26.2 us: accumulate(): token_block[:, local_rows]]
    reduce_scatter x2 -> x0, waiting for transfers between devices: 57.3 us -> none  [the longest x1 57.3 us: on_device(): lax.psum_scatter(sparse_apply(full_tokens, live_tiles, local_rows, local_...]
    scatter-add x1 -> x0, other arithmetic: 52.9 us -> none  [tile_grads(): jnp.zeros((row_blocks * col_blocks, TILE, TILE), jnp.float32).at[slot_ids]]
    all_to_all x0 -> x1, blocking collectives: none -> 39.4 us  [exchange_sum(): lax.all_to_all(partial.reshape(n, rows, partial.shape[1]), axis, split_ax...]
    mul x2 -> x0, other arithmetic: 19.1 us -> none  [the longest x1 11.8 us: tile_grads(): tile_sums = tile_sums * is_live[:, None, None].astype(jnp.float32)]
    unnamed x16 -> x8, local copies, waits for them, and re-layouts: 26.8 us -> 44.3 us
  transfers between devices with their start and end apart: 4 -> 3, of which waited for: 3 -> 2; matrix products, arithmetic and copies ran while one was open for 38% -> 28% of each run, Pallas kernels for 0% -> 0%
where the time goes in v1:
time: 232 us; the launch traced here: 231 us
  local copies, waits for them, and re-layouts  71.6 us (31%)
  waiting for transfers between devices  49.8 us (21%)
  matrix products  45 us (19%)
  blocking collectives  39.4 us (17%)
  between operations  14.8 us (6%)
  starting transfers between devices  5.59 us (2%)
  other arithmetic  4.66 us (2%)
    unnamed x8, local copies, waits for them, and re-layouts  44.3 us
    all_to_all x1, blocking collectives, exchange_sum(): lax.all_to_all(partial.reshape(n, rows, partial.shape[1]), axis, split_ax...  39.4 us
    broadcast_in_dim x1, local copies, waits for them, and re-layouts, on_device(): jnp.where(live, shaped, jnp.zeros_like(shaped)).reshape(weight.shape)  26.5 us
    all_gather x1, waiting for transfers between devices, on_device(): full_grads = lax.all_gather(grad_pre, 'col', axis=0, tiled=True)  26.1 us
    all_gather x1, waiting for transfers between devices, on_device(): full_tokens = lax.all_gather(tokens, 'row', axis=0, tiled=True)  23 us
    dot_general x1, matrix products, on_device(): lax.dot_general(full_tokens, full_grads, (((0,), (0,)), ((), ())), prefer...  17.3 us
    dot_general x1, matrix products, on_device(): partial = jnp.dot(full_tokens, masked, preferred_element_type=jnp.float32)  13.5 us
    dot_general x1, matrix products, on_device(): lax.dot_general(full_grads, masked, (((1,), (1,)), ((), ())), preferred_e...  13.5 us
  transfers between devices with their start and end apart: 3, of which 2 were waited for; matrix products, arithmetic and copies ran while one was open for 28% of the time, Pallas kernels for 0%

profile of v1, /device:TPU:0, one launch (start us, length us, event | category | flops | bytes accessed | tf_op | source)
XLA Modules:
  0.0 230.9 jit_solution(18191495320413865887)
XLA Ops:
  7.2 0.0 all-gather.3.cloned.1.call-start
  7.2 0.7 all-gather.3.cloned.1.call-update
  7.9 0.0 all-gather.5.cloned.1.call-start
  8.6 0.7 broadcast_subtract_fusion.1
  9.3 0.7 broadcast_subtract_fusion
  10.0 0.8 convolution_compare_fusion
  10.8 0.8 copy.9
  11.6 22.5 %copy.10 = bf16[2048,4096]{0,1:T(8,128)(2,1)} copy(bf16[2048,4096]{1,0:T(8,128)(2,1)} %param.7) | data formatting | bytes 33554432 | tf_op args[1]
  34.1 23.0 %all-gather.3.cloned.1.call-done = bf16[384,2048]{1,0:T(8,128)(2,1)} async-done(((bf16[48,2048]{1,0:T(8,128)(2,1)}), bf16[384,2048]{1,0:T(8,128)(2,1)}) %all-gather.3.cloned.1.call-update) | async-done | bytes 1572880 | tf_op jit(solution)/shard_map/all_gather | solution.py:38
  57.1 0.0 copy-start.2
  57.1 26.5 %broadcast_in_dim.29 = pred[16,128,4096]{1,0,2:T(8,128)(4,1)S(1)} broadcast(pred[16,4096]{0,1:T(8,128)(4,1)S(1)} %copy.9), dimensions={0,2} | broadcast | bytes 8454144 | tf_op jit(solution)/shard_map/jit(_where)/broadcast_in_dim | solution.py:36
  83.6 0.0 copy-start
  83.6 0.0 copy-done.2
  83.6 13.5 %fusion.5 = bf16[4096,384]{0,1:T(8,128)(2,1)S(1)} fusion(bf16[384,2048]{1,0:T(8,128)(2,1)S(1)} %copy-done.2, bf16[2048,4096]{0,1:T(8,128)(2,1)} %copy.10, pred[512,8,16,128]{3,2,1,0:T(8,128)(4,1)S(1)} %bitcast.28), kind=kOutput, calls=%fused_computation.8 | convolution fusion | flops 6452412416 | bytes 29884416 | tf_op jit(solution)/shard_map/dot_general | solution.py:39
  97.2 0.0 copy-done
  97.2 39.4 %all_to_all.10 = bf16[4,96,4096]{2,1,0:T(8,128)(2,1)S(1)} all-to-all(bf16[4,96,4096]{2,1,0:T(8,128)(2,1)S(1)} %bitcast.31), channel_id=1, replica_groups=mesh['row'=8,'col'=4] {'col'}, dimensions={0} | all-to-all | bytes 6291456 | tf_op jit(solution)/shard_map/all_to_all | solution.py:12
  136.6 0.0 copy-start.1
  136.6 0.5 convert_reduce_fusion
  137.1 0.6 copy-done.1
  137.8 1.8 multiply_convert_fusion
  139.6 0.0 all-gather.5.cloned.1.call-update
  139.6 26.1 %all-gather.5.cloned.1.call-done = bf16[384,4096]{1,0:T(8,128)(2,1)} async-done(((bf16[96,4096]{1,0:T(8,128)(2,1)}), bf16[384,4096]{1,0:T(8,128)(2,1)}) %all-gather.5.cloned.1.call-update) | async-done | bytes 3145744 | tf_op jit(solution)/shard_map/all_gather | solution.py:45
  165.7 13.5 %fusion.7 = bf16[384,2048]{1,0:T(8,128)(2,1)} fusion(bf16[384,4096]{1,0:T(8,128)(2,1)} %all-gather.5.cloned.1.call-done, bf16[2048,4096]{0,1:T(8,128)(2,1)} %copy.10, pred[512,8,16,128]{3,2,1,0:T(8,128)(4,1)} %bitcast.29), kind=kOutput, calls=%fused_computation.11 | convolution fusion | flops 6451625984 | bytes 29884416 | tf_op jit(solution)/shard_map/dot_general | solution.py:46
  179.2 5.5 %all-to-all-start.1 = ((bf16[8,48,2048]{2,1,0:T(8,128)(2,1)}), bf16[8,48,2048]{2,1,0:T(8,128)(2,1)S(1)}, u32[]{:S(2)}, u32[]{:S(2)}) async-start(bf16[8,48,2048]{2,1,0:T(8,128)(2,1)} %bitcast.5), calls=%async_computation.1 | async-start | bytes 3145728 | tf_op jit(solution)/shard_map/all_to_all | solution.py:12
  184.7 17.3 %fusion = bf16[2048,4096]{0,1:T(8,128)(2,1)} fusion(pred[512,8,16,128]{3,2,1,0:T(8,128)(4,1)} %bitcast.30, bf16[384,4096]{1,0:T(8,128)(2,1)} %all-gather.5.cloned.1.call-done, bf16[384,2048]{1,0:T(8,128)(2,1)S(1)} %copy-done.2), kind=kOutput, calls=%fused_computation.1 | convolution fusion | flops 6459228160 | bytes 29884416 | tf_op jit(solution)/shard_map/dot_general | solution.py:50
  201.9 21.2 %copy.11 = bf16[2048,4096]{1,0:T(8,128)(2,1)} copy(bf16[2048,4096]{0,1:T(8,128)(2,1)} %fusion) | data formatting | bytes 33554432
  223.1 0.0 all-to-all-done.1
  223.1 0.9 reduce_sum.22
  (2 shorter events, 0.0 us)
Async XLA Ops:
  7.2 49.9 %all-gather.3.cloned.1.call-start = ((), (), s32[]{:S(2)}) async-start(), calls=%async_computation.2 | async-start | bytes 1769472 | tf_op jit(solution)/shard_map/all_gather | solution.py:38
  7.9 157.8 %all-gather.5.cloned.1.call-start = ((), (), s32[]{:S(2)}) async-start(), calls=%async_computation.3 | async-start | bytes 3932160 | tf_op jit(solution)/shard_map/all_gather | solution.py:45
  57.1 26.5 %copy-start.2 = (bf16[384,2048]{1,0:T(8,128)(2,1)S(1)}, bf16[384,2048]{1,0:T(8,128)(2,1)}, u32[]{:S(2)}) copy-start(bf16[384,2048]{1,0:T(8,128)(2,1)} %all-gather.3.cloned.1.call-done) | copy-start | bytes 4718596
  83.6 13.6 %copy-start = (pred[16,128,4096]{1,0,2:T(8,128)(4,1)}, pred[16,128,4096]{1,0,2:T(8,128)(4,1)S(1)}, u32[]{:S(2)}) copy-start(pred[16,128,4096]{1,0,2:T(8,128)(4,1)S(1)} %broadcast_in_dim.29) | copy-start | bytes 25165828
  136.6 1.1 copy-start.1
  179.2 44.0 %all-to-all-start.1 = ((bf16[8,48,2048]{2,1,0:T(8,128)(2,1)}), bf16[8,48,2048]{2,1,0:T(8,128)(2,1)S(1)}, u32[]{:S(2)}, u32[]{:S(2)}) async-start(bf16[8,48,2048]{2,1,0:T(8,128)(2,1)} %bitcast.5), calls=%async_computation.1 | async-start | bytes 3145728 | tf_op jit(solution)/shard_map/all_to_all | solution.py:12
Sparse Core Ops, SparseCore 0:
  10.2 46.8 all-gather.2
  139.7 25.9 all-gather.4

commit v2 on v1

--- a/solution.py
+++ b/solution.py
@@ -1,6 +1,8 @@
 import jax
 import jax.numpy as jnp
 from jax import lax
+from jax.experimental import pallas as pl
+from jax.experimental.pallas import tpu as pltpu
 from jax.sharding import PartitionSpec as P
 
 TILE = 128
@@ -13,6 +15,110 @@
         partial.reshape(n, rows, partial.shape[1]), axis, split_axis=0, concat_axis=0
     )
     return mine.astype(jnp.float32).sum(axis=0)
+
+
+def paired_exchange_sum(partial, axis):
+    n = lax.psum(1, axis)
+    if n % 2:
+        return exchange_sum(partial, axis)
+    chips = n // 2
+    rows = partial.shape[0] // n
+    here = lax.axis_index(axis)
+    chip, core = here // 2, here % 2
+    blocks = partial.reshape(chips, 2, rows, partial.shape[1])
+    away = lax.dynamic_index_in_dim(blocks, 1 - core, 1, keepdims=False)
+    keep = lax.dynamic_index_in_dim(blocks, core, 1, keepdims=False)
+    came = lax.ppermute(away, axis, [(i, i ^ 1) for i in range(n)])
+
+    def pair_block(which):
+        ours = lax.dynamic_index_in_dim(keep, which, 0, keepdims=False)
+        theirs = lax.dynamic_index_in_dim(came, which, 0, keepdims=False)
+        return ours.astype(jnp.float32) + theirs.astype(jnp.float32)
+
+    arrived = [
+        lax.ppermute(
+            pair_block((chip + step) % chips).astype(jnp.bfloat16),
+            axis,
+            [(i, (i + 2 * step) % n) for i in range(n)],
+        )
+        for step in range(1, chips)
+    ]
+    total = pair_block(chip)
+    for block in arrived:
+        total = total + block.astype(jnp.float32)
+    return total
+
+
+def mask_weight(mask_ref, weight_ref, held):
+    for block in range(mask_ref.shape[0]):
+        rows = pl.ds(block * TILE, TILE)
+        tile = weight_ref[rows, :]
+        live = jnp.broadcast_to(mask_ref[block : block + 1, :], tile.shape) > 0.5
+        held[rows, :] = jnp.where(live, tile.astype(jnp.float32), 0.0).astype(jnp.bfloat16)
+
+
+def forward_kernel(mask_ref, tokens_ref, weight_ref, out_ref, held):
+    mask_weight(mask_ref, weight_ref, held)
+    out_ref[...] = jnp.dot(
+        tokens_ref[...], held[...], preferred_element_type=jnp.float32
+    ).astype(jnp.bfloat16)
+
+
+def backward_kernel(mask_ref, grads_ref, weight_ref, out_ref, held, total):
+    step = pl.program_id(0)
+    mask_weight(mask_ref, weight_ref, held)
+    product = lax.dot_general(
+        grads_ref[...], held[...], (((1,), (1,)), ((), ())), preferred_element_type=jnp.float32
+    )
+
+    @pl.when(step == 0)
+    def _():
+        total[...] = product
+
+    @pl.when(step > 0)
+    def _():
+        total[...] += product
+
+    @pl.when(step == pl.num_programs(0) - 1)
+    def _():
+        out_ref[...] = total[...].astype(jnp.bfloat16)
+
+
+def weight_kernel(mask_ref, turned_ref, grads_ref, out_ref):
+    for block in range(mask_ref.shape[0]):
+        rows = pl.ds(block * TILE, TILE)
+        product = jnp.dot(
+            turned_ref[rows, :], grads_ref[...], preferred_element_type=jnp.float32
+        )
+        live = jnp.broadcast_to(mask_ref[block : block + 1, :], product.shape) > 0.5
+        out_ref[rows, :] = jnp.where(live, product, 0.0).astype(jnp.bfloat16)
+
+
+def run(kernel, mask, left, right, width, left_blocked, out, out_blocked, scratch):
+    blocks, total_width = mask.shape
+    depth = blocks * TILE
+    column = lambda rows: pl.BlockSpec((rows, width), lambda i: (0, i))
+    whole = lambda shape: pl.BlockSpec(shape, lambda i: (0, 0))
+    moved = sum(a.size * a.dtype.itemsize for a in (left, right)) + out[0] * out[1] * 2
+    count = left.shape[1] if kernel is weight_kernel else left.shape[0]
+    return pl.pallas_call(
+        kernel,
+        grid=(total_width // width,),
+        in_specs=[
+            column(blocks),
+            column(left.shape[0]) if left_blocked else whole(left.shape),
+            column(right.shape[0]),
+        ],
+        out_specs=column(out[0]) if out_blocked else whole(out),
+        out_shape=jax.ShapeDtypeStruct(out, jnp.bfloat16),
+        scratch_shapes=scratch,
+        cost_estimate=pl.CostEstimate(
+            flops=2 * count * depth * total_width, bytes_accessed=moved, transcendentals=0
+        ),
+        compiler_params=pltpu.CompilerParams(
+            dimension_semantics=("arbitrary",), vmem_limit_bytes=48 * 1024 * 1024
+        ),
+    )(mask, left, right)
 
 
 def on_device(tokens, weight, tile_rows, tile_cols, tile_count, hidden_cotangent):
@@ -31,26 +137,31 @@
         jnp.bfloat16
     )
     mask = jnp.dot(row_pick, col_pick, preferred_element_type=jnp.float32)
-    live = (mask > 0.5)[:, None, :]
-    shaped = weight.reshape(row_blocks, TILE, weight.shape[1])
-    masked = jnp.where(live, shaped, jnp.zeros_like(shaped)).reshape(weight.shape)
+    width = min(512, weight.shape[1])
+    held = pltpu.VMEM((weight.shape[0], width), jnp.bfloat16)
 
     full_tokens = lax.all_gather(tokens, "row", axis=0, tiled=True)
-    partial = jnp.dot(full_tokens, masked, preferred_element_type=jnp.float32)
-    pre_act = exchange_sum(partial.astype(jnp.bfloat16), "col")
+    count = full_tokens.shape[0]
+    partial = run(
+        forward_kernel, mask, full_tokens, weight, width, False,
+        (count, weight.shape[1]), True, [held],
+    )
+    pre_act = paired_exchange_sum(partial, "col")
     gate_value = jax.nn.sigmoid(pre_act)
     hidden = (pre_act * gate_value).astype(jnp.bfloat16)
     silu_slope = gate_value * (1.0 + pre_act * (1.0 - gate_value))
     grad_pre = (hidden_cotangent.astype(jnp.float32) * silu_slope).astype(jnp.bfloat16)
     full_grads = lax.all_gather(grad_pre, "col", axis=0, tiled=True)
-    share = lax.dot_general(
-        full_grads, masked, (((1,), (1,)), ((), ())), preferred_element_type=jnp.float32
+    share_shape = (count, weight.shape[0])
+    share = run(
+        backward_kernel, mask, full_grads, weight, width, True,
+        share_shape, False, [held, pltpu.VMEM(share_shape, jnp.float32)],
     )
-    input_grad = exchange_sum(share.astype(jnp.bfloat16), "row").astype(jnp.bfloat16)
-    full = lax.dot_general(
-        full_tokens, full_grads, (((0,), (0,)), ((), ())), preferred_element_type=jnp.float32
-    ).reshape(row_blocks, TILE, weight.shape[1])
-    weight_grad = jnp.where(live, full, 0.0).astype(jnp.bfloat16).reshape(weight.shape)
+    input_grad = exchange_sum(share, "row").astype(jnp.bfloat16)
+    weight_grad = run(
+        weight_kernel, mask, full_tokens.T, full_grads, width, False,
+        weight.shape, True, [],
+    )
     return (hidden, input_grad, weight_grad)
 
 

time: 232 us -> 197 us (0.85)
  waiting for transfers between devices: 49.8 us -> 119 us
  local copies, waits for them, and re-layouts: 71.6 us -> 7.3 us
  matrix products: 45 us -> 0.8 us
  blocking collectives: 39.4 us -> 0 us
  Pallas kernels: 0 us -> 38 us
  other arithmetic: 4.66 us -> 9.56 us
    dot_general x3 -> x0, matrix products: 44.2 us -> none  [the longest x1 17.3 us: on_device(): lax.dot_general(full_tokens, full_grads, (((0,), (0,)), ((), ())), prefer...]
    all_to_all x1 -> x0, blocking collectives: 39.4 us -> none  [exchange_sum(): lax.all_to_all(partial.reshape(n, rows, partial.shape[1]), axis, split_ax...]
    unnamed x8, local copies, waits for them, and re-layouts: 44.3 us -> 5.18 us
    pallas_call x0 -> x3, Pallas kernels: none -> 38 us  [run(): pl.pallas_call(kernel, grid=(total_width // width,), in_specs=[column(blo...]
    broadcast_in_dim x1 -> x0, local copies, waits for them, and re-layouts: 26.5 us -> none  [on_device(): jnp.where(live, shaped, jnp.zeros_like(shaped)).reshape(weight.shape)]
    all_gather x1, waiting for transfers between devices: 23 us -> 46.3 us  [on_device(): full_tokens = lax.all_gather(tokens, 'row', axis=0, tiled=True)]
    all_to_all x1, waiting for transfers between devices: 0.01 us -> 23 us  [exchange_sum(): lax.all_to_all(partial.reshape(n, rows, partial.shape[1]), axis, split_ax...]
    ppermute x0 -> x2, waiting for transfers between devices: none -> 22.2 us  [the longest x1 18.4 us: paired_exchange_sum(): lax.ppermute(pair_block((chip + step) % chips).astype(jnp.bfloat16), axis...]
  transfers between devices with their start and end apart: 3 -> 5, of which waited for: 2 -> 5; matrix products, arithmetic and copies ran while one was open for 28% -> 2% of each run, Pallas kernels for 0% -> 6%
where the time goes in v2:
time: 197 us
  waiting for transfers between devices  119 us (60%)
  Pallas kernels  38 us (19%)
  between operations  14.8 us (8%)
  other arithmetic  9.56 us (5%)
  local copies, waits for them, and re-layouts  7.3 us (4%)
  starting transfers between devices  7.19 us (4%)
    all_gather x1, waiting for transfers between devices, on_device(): full_tokens = lax.all_gather(tokens, 'row', axis=0, tiled=True)  46.3 us
    pallas_call x3, Pallas kernels, run(): pl.pallas_call(kernel, grid=(total_width // width,), in_specs=[column(blo...  38 us
    all_gather x1, waiting for transfers between devices, on_device(): full_grads = lax.all_gather(grad_pre, 'col', axis=0, tiled=True)  27 us
    all_to_all x1, waiting for transfers between devices, exchange_sum(): lax.all_to_all(partial.reshape(n, rows, partial.shape[1]), axis, split_ax...  23 us
    ppermute x1, waiting for transfers between devices, paired_exchange_sum(): lax.ppermute(pair_block((chip + step) % chips).astype(jnp.bfloat16), axis...  18.4 us
    all_to_all x1, starting transfers between devices, exchange_sum(): lax.all_to_all(partial.reshape(n, rows, partial.shape[1]), axis, split_ax...  5.65 us
    unnamed x8, local copies, waits for them, and re-layouts  5.18 us
  transfers between devices with their start and end apart: 5, of which 5 were waited for; matrix products, arithmetic and copies ran while one was open for 2% of the time, Pallas kernels for 6%

profile of v2, /device:TPU:0, one launch (start us, length us, event | category | flops | bytes accessed | tf_op | source)
XLA Modules:
  0.0 196.8 jit_solution(5473653634758635045)
XLA Ops:
  7.2 0.0 all-gather.3.cloned.1.call-start
  7.2 0.7 all-gather.3.cloned.1.call-update
  7.9 0.0 all-gather.5.cloned.1.call-start
  8.6 0.7 broadcast_subtract_fusion.1
  9.3 0.7 broadcast_subtract_fusion
  10.0 0.8 fusion.mask_ref
  10.8 46.3 %all-gather.3.cloned.1.call-done.tokens_ref = bf16[384,2048]{1,0:T(8,128)(2,1)} async-done(((bf16[48,2048]{1,0:T(8,128)(2,1)}), bf16[384,2048]{1,0:T(8,128)(2,1)}) %all-gather.3.cloned.1.call-update) | async-done | bytes 1572880 | tf_op jit(solution)/shard_map/all_gather | solution.py:143
  57.1 0.0 copy-start
  57.1 1.4 copy-done
  58.5 11.8 %shard_map.85 = bf16[384,4096]{1,0:T(8,128)(2,1)S(1)} custom-call(f32[16,4096]{1,0:T(8,128)S(1)} %fusion.mask_ref, bf16[384,2048]{1,0:T(8,128)(2,1)S(1)} %copy-done, bf16[2048,4096]{1,0:T(8,128)(2,1)} %weight_ref.3), custom_call_target="tpu_custom_call" | custom-call | flops 6442450944 | bytes 21495808 | tf_op jit(solution)/shard_map/pallas_call | solution.py:104
  70.3 1.3 dynamic-slice_bitcast_fusion
  71.5 0.0 collective-permute-start
  71.5 3.7 %collective-permute-done = bf16[2,96,4096]{2,1,0:T(8,128)(2,1)} collective-permute-done((bf16[2,96,4096]{2,1,0:T(8,128)(2,1)}, bf16[2,96,4096]{2,1,0:T(8,128)(2,1)}, u32[]{:S(2)}, u32[]{:S(2)}) %collective-permute-start) | collective-permute-done | bytes 1572896 | tf_op jit(solution)/shard_map/ppermute | solution.py:31
  75.3 2.2 %fusion.4 = bf16[96,4096]{1,0:T(8,128)(2,1)} fusion(bf16[2,96,4096]{2,1,0:T(8,128)(2,1)} %collective-permute-done, s32[]{:T(128)S(6)} %select_n.55, bf16[2,2,96,4096]{3,2,1,0:T(8,128)(2,1)S(1)} %bitcast.24, s32[]{:T(128)S(6)} %select_n.56, s32[]{:T(128)S(6)} %select_n.52), kind=kLoop, calls=%fused_computation.5 | loop fusion | flops 1572864 | bytes 2359308 | tf_op jit(solution)/shard_map/convert_element_type | solution.py:40
  77.5 1.5 collective-permute-start.1
  78.9 18.4 %collective-permute-done.1 = bf16[96,4096]{1,0:T(8,128)(2,1)} collective-permute-done((bf16[96,4096]{1,0:T(8,128)(2,1)}, bf16[96,4096]{1,0:T(8,128)(2,1)}, u32[]{:S(2)}, u32[]{:S(2)}) %collective-permute-start.1) | collective-permute-done | bytes 786464 | tf_op jit(solution)/shard_map/ppermute | solution.py:39
  97.4 3.6 %multiply_convert_fusion = (bf16[96,4096]{1,0:T(8,128)(2,1)}, bf16[96,4096]{1,0:T(8,128)(2,1)}) fusion(bf16[96,4096]{1,0:T(8,128)(2,1)} %param.11, bf16[96,4096]{1,0:T(8,128)(2,1)} %collective-permute-done.1, bf16[2,96,4096]{2,1,0:T(8,128)(2,1)} %collective-permute-done, s32[]{:T(128)S(6)} %select_n.48, bf16[2,2,96,4096]{3,2,1,0:T(8,128)(2,1)S(1)} %bitcast.25, ...), kind=kLoop, calls=%fused_computation.8 | loop fusion | flops 6684672 | bytes 4718604 | tf_op jit(solution)/shard_map/convert_element_type | solution.py:153
  101.0 0.0 all-gather.5.cloned.1.call-update
  101.0 27.0 %all-gather.5.cloned.1.call-done.grads_ref = bf16[384,4096]{1,0:T(8,128)(2,1)} async-done(((bf16[96,4096]{1,0:T(8,128)(2,1)}), bf16[384,4096]{1,0:T(8,128)(2,1)}) %all-gather.5.cloned.1.call-update) | async-done | bytes 3145744 | tf_op jit(solution)/shard_map/all_gather | solution.py:154
  128.0 0.0 copy-start.2
  128.0 1.9 copy-done.2
  129.9 14.5 %shard_map.86 = bf16[384,2048]{1,0:T(8,128)(2,1)} custom-call(f32[16,4096]{1,0:T(8,128)S(1)} %fusion.mask_ref, bf16[384,4096]{1,0:T(8,128)(2,1)S(1)} %copy-done.2, bf16[2048,4096]{1,0:T(8,128)(2,1)} %weight_ref.3), custom_call_target="tpu_custom_call" | custom-call | flops 6442450944 | bytes 21495808 | tf_op jit(solution)/shard_map/pallas_call | solution.py:104
  144.4 0.0 copy-start.1
  144.4 5.6 %all-to-all-start = ((bf16[8,48,2048]{2,1,0:T(8,128)(2,1)}), bf16[8,48,2048]{2,1,0:T(8,128)(2,1)}, u32[]{:S(2)}, u32[]{:S(2)}) async-start(bf16[8,48,2048]{2,1,0:T(8,128)(2,1)} %bitcast.9), calls=%async_computation | async-start | bytes 3145728 | tf_op jit(solution)/shard_map/all_to_all | solution.py:14
  150.0 0.0 copy-done.1
  150.0 0.9 copy.11
  150.9 0.0 copy-start.3
  150.9 1.9 copy-done.3
  152.8 11.8 %shard_map.87 = bf16[2048,4096]{1,0:T(8,128)(2,1)} custom-call(f32[16,4096]{1,0:T(8,128)S(1)} %fusion.mask_ref, bf16[2048,384]{1,0:T(8,128)(2,1)S(1)} %bitcast.26, bf16[384,4096]{1,0:T(8,128)(2,1)S(1)} %copy-done.3), custom_call_target="tpu_custom_call" | custom-call | flops 6442450944 | bytes 21495808 | tf_op jit(solution)/shard_map/pallas_call | solution.py:104
  164.6 23.0 %all-to-all-done = bf16[8,48,2048]{2,1,0:T(8,128)(2,1)} async-done(((bf16[8,48,2048]{2,1,0:T(8,128)(2,1)}), bf16[8,48,2048]{2,1,0:T(8,128)(2,1)}, u32[]{:S(2)}, u32[]{:S(2)}) %all-to-all-start) | async-done | bytes 1572896 | tf_op jit(solution)/shard_map/all_to_all | solution.py:14
  187.5 2.4 %reduce_sum.12 = bf16[48,2048]{1,0:T(8,128)(2,1)} reduce(bf16[8,48,2048]{2,1,0:T(8,128)(2,1)} %all-to-all-done, bf16[]{:T(256)} %constant.119.clone.1), dimensions={0}, to_apply=%region_0.1 | reduce | flops 688128 | bytes 1769474 | tf_op jit(solution)/shard_map/reduce_sum | solution.py:17
  (2 shorter events, 0.0 us)
Async XLA Ops:
  7.2 49.9 %all-gather.3.cloned.1.call-start = ((), (), s32[]{:S(2)}) async-start(), calls=%async_computation.1 | async-start | bytes 1769472 | tf_op jit(solution)/shard_map/all_gather | solution.py:143
  7.9 120.1 %all-gather.5.cloned.1.call-start = ((), (), s32[]{:S(2)}) async-start(), calls=%async_computation.2 | async-start | bytes 3932160 | tf_op jit(solution)/shard_map/all_gather | solution.py:154
  57.1 1.4 copy-start
  71.5 3.8 %collective-permute-start = (bf16[2,96,4096]{2,1,0:T(8,128)(2,1)}, bf16[2,96,4096]{2,1,0:T(8,128)(2,1)}, u32[]{:S(2)}, u32[]{:S(2)}) collective-permute-start(bf16[2,96,4096]{2,1,0:T(8,128)(2,1)} %dynamic-slice_bitcast_fusion), channel_id=1, source_target_pairs={{0,1},{1,0},{2,3},{3,2},{4,5},{5,4},{6,7},{7,6},{8,9},{9,8},{10,11... | collective-permute-start | bytes 4718600 | tf_op jit(solution)/shard_map/ppermute | solution.py:31
  77.5 19.9 %collective-permute-start.1 = (bf16[96,4096]{1,0:T(8,128)(2,1)}, bf16[96,4096]{1,0:T(8,128)(2,1)}, u32[]{:S(2)}, u32[]{:S(2)}) collective-permute-start(bf16[96,4096]{1,0:T(8,128)(2,1)} %fusion.4), channel_id=1, source_target_pairs={{0,2},{1,3},{2,0},{3,1},{4,6},{5,7},{6,4},{7,5},{8,10},{9,11},{10,... | collective-permute-start | bytes 2359304 | tf_op jit(solution)/shard_map/ppermute | solution.py:39
  128.0 1.9 copy-start.2
  144.4 5.7 %copy-start.1 = (bf16[384,2048]{1,0:T(8,128)(2,1)S(1)}, bf16[384,2048]{1,0:T(8,128)(2,1)}, u32[]{:S(2)}) copy-start(bf16[384,2048]{1,0:T(8,128)(2,1)} %all-gather.3.cloned.1.call-done.tokens_ref) | copy-start | bytes 4718596
  144.4 43.2 %all-to-all-start = ((bf16[8,48,2048]{2,1,0:T(8,128)(2,1)}), bf16[8,48,2048]{2,1,0:T(8,128)(2,1)}, u32[]{:S(2)}, u32[]{:S(2)}) async-start(bf16[8,48,2048]{2,1,0:T(8,128)(2,1)} %bitcast.9), calls=%async_computation | async-start | bytes 3145728 | tf_op jit(solution)/shard_map/all_to_all | solution.py:14
  150.9 1.9 copy-start.3
Sparse Core Ops, SparseCore 0:
  10.2 46.8 all-gather.2
  101.1 26.8 all-gather.4
